TPU v7x, 32 devices: a whole 2x2x4 slice. The times are simulated.
32 devices in a mesh: groups: 2 (over x), ep: 16 (over z, y, core).
Axes of the slice: x: 2, y: 2, z: 4, core: 2. Of those that a mesh axis runs over, the one named last changes fastest.
Arguments:
- states: float32 [2, 256, 2048], P(None, ('groups', 'ep')), parts along dimension 1, may hold values from -6 to 6
- attn_gain: float32 [2048], replicated, may hold values from 0.1 to 1.9
- moe_gain: float32 [2048], replicated, may hold values from 0.1 to 1.9
- w_query: bfloat16 [2048, 2048], P(None, 'ep'), may hold values from -11 to 11
- w_key: bfloat16 [2048, 256], P(None, 'ep'), may hold values from -0.125 to 0.125
- w_value: bfloat16 [2048, 256], P(None, 'ep'), may hold values from -0.125 to 0.125
- w_output: bfloat16 [2048, 2048], P('ep'), may hold values from -0.125 to 0.125
- w_gate_up: bfloat16 [16, 2048, 1536], P('ep'), may hold values from -0.125 to 0.125
- w_down: bfloat16 [16, 768, 2048], P('ep'), may hold values from -0.21875 to 0.21875
- key_cache: bfloat16 [64, 1024, 256], P(('groups', 'ep')), parts along dimension 0, may hold values from -60 to 60
- value_cache: bfloat16 [64, 1024, 256], P(('groups', 'ep')), parts along dimension 0, may hold values from -24 to 24
- cache_lengths: int32 [64], P(('groups', 'ep')), parts along dimension 0, may hold values from 1 to 1024, as said below
- prefix_slot: int32 [256], P(('groups', 'ep')), parts along dimension 0, may hold values from 0 to 1
- routes: int32 [256, 2, 8], P(('groups', 'ep')), parts along dimension 0, may hold values from 0 to 15, all different within a row; in each aligned block of 16 rows (0 to 15, 16 to 31, ..., all dimensions but the last counted through in order) at most 16 rows name the same one
- gate_weights: float32 [2, 256, 8], P(None, ('groups', 'ep')), parts along dimension 1, may hold values from 0.05 to 0.5
Outputs:
- layer_out: float32 [2, 256, 2048], P(None, ('groups', 'ep')), parts along dimension 1
- appended_kv: bfloat16 [2, 256, 512], P(None, ('groups', 'ep')), parts along dimension 1
There are 2 independent parts, one for each index of `groups`. A program takes and returns all parts, laid end to end along the dimension named above; an argument that names none is the same for every part. Nothing has to cross between parts.
Inputs may be any that keep to these rules, and one draw needn't show every extreme that they name: `cache_lengths`: positions beyond a prefix's length are unused; some prefix is full at 1024. `routes`: over both steps together, the 8 branches of one ep device choose any one expert at most 16 times; a branch's 8 experts at one step differ.
All inputs are finite; a program needn't handle non-finite values.
Results may differ from a plain program's by a relative error of at most 0.0024.
The roundings to bfloat16 on the way count: a program that leaves them out, or rounds other values in their place, can miss the bound.
Values may be sent and summed in bfloat16 or wider, within the bound.
A program may use at most 128 MiB of HBM per device.

v0:
```python
import math

import jax
import jax.numpy as jnp
from jax import lax
from jax.sharding import PartitionSpec as P

HQ = 16
KVH = 2
HD = 128
TOPK = 8


EPS = 1e-06
THETA = 1000000.0


def rms_scale(values, gain):
    squares = jnp.mean(values * values, axis=-1, keepdims=True)
    return values * lax.rsqrt(squares + EPS) * gain


def rotate(vectors, positions):
    head_size = vectors.shape[-1]
    half_size = head_size // 2
    inverse_rate = THETA ** (-(jnp.arange(half_size).astype(jnp.float32) * 2.0 / head_size))
    phases = positions[..., None, None] * inverse_rate
    cosine = jnp.cos(phases)
    sine_part = jnp.sin(phases)
    first_half = vectors[..., :half_size]
    second_half = vectors[..., half_size:]
    return jnp.concatenate(
        [
            first_half * cosine - second_half * sine_part,
            second_half * cosine + first_half * sine_part,
        ],
        axis=-1,
    )


def attend_block(queries, new_keys, new_values, key_block, value_block, lengths, slots):
    step_count, row_count, head_count, head_size = queries.shape
    prefix_count, cache_span, kv_heads, _ = key_block.shape
    group_size = head_count // kv_heads
    grouped = queries.reshape(step_count, row_count, kv_heads, group_size, head_size)
    inv_root = 1.0 / math.sqrt(head_size)
    far_scores = (
        jnp.einsum("srkgd,pckd->srkgpc", grouped, key_block, preferred_element_type=jnp.float32)
        * inv_root
    )
    visible = (jnp.arange(cache_span)[None, None, :] < lengths[None, :, None]) & (
        slots[:, None, None] == jnp.arange(prefix_count)[None, :, None]
    )
    far_scores = jnp.where(visible[None, :, None, None], far_scores, -1e30)
    own_scores = (
        jnp.einsum("srkgd,trkd->srkgt", grouped, new_keys, preferred_element_type=jnp.float32)
        * inv_root
    )
    causal = jnp.arange(step_count)[None, :] <= jnp.arange(step_count)[:, None]
    own_scores = jnp.where(causal[:, None, None, None, :], own_scores, -1e30)
    peak = jnp.maximum(jnp.max(far_scores, axis=(-2, -1)), jnp.max(own_scores, axis=-1))
    far_weights = jnp.exp(far_scores - peak[..., None, None])
    own_weights = jnp.exp(own_scores - peak[..., None])
    normalizer = jnp.sum(far_weights, axis=(-2, -1)) + jnp.sum(own_weights, axis=-1)
    far_probs = (far_weights / normalizer[..., None, None]).astype(jnp.bfloat16)
    own_probs = (own_weights / normalizer[..., None]).astype(jnp.bfloat16)
    attended = jnp.einsum(
        "srkgpc,pckd->srkgd", far_probs, value_block, preferred_element_type=jnp.float32
    )
    attended = attended + jnp.einsum(
        "srkgt,trkd->srkgd", own_probs, new_values, preferred_element_type=jnp.float32
    )
    return attended.reshape(step_count, row_count, head_count * head_size).astype(jnp.bfloat16)


def shards(
    states,
    attn_gain,
    moe_gain,
    w_query,
    w_key,
    w_value,
    w_output,
    w_gate_up,
    w_down,
    key_cache,
    value_cache,
    cache_lengths,
    prefix_slot,
    routes,
    gate_weights,
):
    devices = lax.axis_size("ep")
    step_count, row_count, model_width = states.shape
    query_cols = w_query.shape[1]
    kv_cols = w_key.shape[1]
    normed = rms_scale(states, attn_gain).astype(jnp.bfloat16)
    joined = jnp.concatenate([w_query, w_key, w_value], axis=1)
    head_parts = jnp.einsum(
        "srd,dc->src",
        lax.all_gather(normed, "ep", axis=1, tiled=True),
        joined,
        preferred_element_type=jnp.float32,
    )
    own_cols = lax.all_to_all(head_parts, "ep", split_axis=1, concat_axis=2, tiled=True)
    own_cols = own_cols.reshape(step_count, row_count, devices, query_cols + 2 * kv_cols)
    queries = own_cols[..., :query_cols].reshape(step_count, row_count, HQ, HD)
    new_keys = own_cols[..., query_cols : query_cols + kv_cols].reshape(
        step_count, row_count, KVH, HD
    )
    new_values = (
        own_cols[..., query_cols + kv_cols :]
        .reshape(step_count, row_count, KVH, HD)
        .astype(jnp.bfloat16)
    )
    prefix_count, cache_span, _ = key_cache.shape
    lengths_here = jnp.sum(
        jnp.where(
            prefix_slot[:, None] == jnp.arange(prefix_count)[None, :], cache_lengths[None, :], 0
        ),
        axis=1,
    )
    positions = (
        lengths_here.astype(jnp.float32)[None, :]
        + jnp.arange(step_count).astype(jnp.float32)[:, None]
    )
    queries = rotate(queries, positions).astype(jnp.bfloat16)
    new_keys = rotate(new_keys, positions).astype(jnp.bfloat16)
    attended = attend_block(
        queries,
        new_keys,
        new_values,
        key_cache.reshape(prefix_count, cache_span, KVH, HD),
        value_cache.reshape(prefix_count, cache_span, KVH, HD),
        cache_lengths,
        prefix_slot,
    )
    w_columns = lax.all_to_all(w_output, "ep", split_axis=1, concat_axis=0, tiled=True)
    column_part = jnp.einsum(
        "srf,fc->src",
        lax.all_gather(attended, "ep", axis=1, tiled=True),
        w_columns,
        preferred_element_type=jnp.float32,
    )
    projected = lax.all_to_all(column_part, "ep", split_axis=1, concat_axis=2, tiled=True)
    hidden = states + projected
    moe_input = (
        rms_scale(hidden, moe_gain)
        .astype(jnp.bfloat16)
        .reshape(step_count * row_count, model_width)
    )
    expert_count = w_gate_up.shape[0] * devices
    capacity = max(2, 4 * row_count * TOPK // expert_count)
    flat_routes = jnp.swapaxes(routes, 0, 1).reshape(-1)
    onehot = (flat_routes[:, None] == jnp.arange(expert_count)[None, :]).astype(jnp.int32)
    running = jnp.cumsum(onehot, axis=0) - 1
    within = jnp.sum(onehot * running, axis=1)
    slot_index = flat_routes * capacity + within
    dispatch = (jnp.arange(expert_count * capacity)[:, None] == slot_index[None, :]).astype(
        jnp.bfloat16
    )
    repeated = jnp.repeat(moe_input, TOPK, axis=0)
    outgoing = jnp.dot(dispatch, repeated, preferred_element_type=jnp.float32).astype(jnp.bfloat16)
    outgoing = outgoing.reshape(expert_count, capacity, model_width)
    both = jnp.einsum(
        "nsd,df->nsf",
        lax.all_to_all(outgoing, "ep", split_axis=0, concat_axis=0, tiled=True),
        w_gate_up[0],
        preferred_element_type=jnp.float32,
    )
    half_cols = both.shape[-1] // 2
    activation = (jax.nn.silu(both[..., :half_cols]) * both[..., half_cols:]).astype(jnp.bfloat16)
    expert_done = jnp.einsum(
        "nsf,fd->nsd", activation, w_down[0], preferred_element_type=jnp.float32
    ).astype(jnp.bfloat16)
    returned = lax.all_to_all(expert_done, "ep", split_axis=0, concat_axis=0, tiled=True)
    picked = returned.reshape(expert_count * capacity, model_width)[slot_index]
    picked = picked.astype(jnp.float32).reshape(step_count, row_count, TOPK, model_width)
    mixture = jnp.sum(gate_weights[..., None] * picked, axis=2)
    appended = jnp.concatenate(
        [
            new_keys.reshape(step_count, row_count, KVH * HD),
            new_values.reshape(step_count, row_count, KVH * HD),
        ],
        axis=-1,
    )
    return (hidden + mixture, appended)


def solution(mesh):
    return jax.shard_map(
        shards,
        mesh=mesh,
        in_specs=(
            P(None, ("groups", "ep"), None),
            P(),
            P(),
            P(None, "ep"),
            P(None, "ep"),
            P(None, "ep"),
            P("ep", None),
            P("ep", None, None),
            P("ep", None, None),
            P(("groups", "ep"), None, None),
            P(("groups", "ep"), None, None),
            P(("groups", "ep")),
            P(("groups", "ep")),
            P(("groups", "ep"), None, None),
            P(None, ("groups", "ep"), None),
        ),
        out_specs=(P(None, ("groups", "ep"), None), P(None, ("groups", "ep"), None)),
        check_vma=False,
    )
```

profile of v0, /device:TPU:0, one launch (start us, length us, event | category | flops | bytes accessed | tf_op | source)
XLA Modules:
  0.0 203.6 jit_solution(11933007128233373446)
XLA Ops:
  7.2 1.2 multiply_reduce_fusion.1
  8.4 1.6 multiply_convert_fusion.1
  10.0 2.0 %copy.137 = bf16[2048,128]{0,1:T(8,128)(2,1)} copy(bf16[2048,128]{1,0:T(8,128)(2,1)} %param.18) | data formatting | bytes 1048576 | tf_op args[3]
  12.1 0.9 select_reduce_fusion.1
  13.0 0.1 multiply_cosine_fusion
  13.2 2.2 %reshape.240 = bf16[2,1024,2,128]{3,2,1,0:T(2,128)(2,1)} reshape(bf16[2,1024,256]{2,1,0:T(8,128)(2,1)} %param.24) | data formatting | bytes 2097152 | tf_op jit(solution)/shard_map/reshape | solution.py:133
  15.5 2.1 %reshape.242 = bf16[2,1024,2,128]{3,2,1,0:T(2,128)(2,1)} reshape(bf16[2,1024,256]{2,1,0:T(8,128)(2,1)} %param.25) | data formatting | bytes 2097152 | tf_op jit(solution)/shard_map/reshape | solution.py:134
  17.8 33.7 %all-gather.3.cloned.1.call-done = bf16[2,128,2048]{2,1,0:T(8,128)(2,1)} async-done(((bf16[2,8,2048]{2,1,0:T(8,128)(2,1)}), bf16[2,128,2048]{2,1,0:T(8,128)(2,1)}) %all-gather.3.cloned.1.call-update) | async-done | bytes 1048592 | tf_op jit(solution)/shard_map/all_gather | solution.py:101
  51.5 1.9 fusion.19
  53.3 0.9 copy.138
  54.2 3.6 %all-to-all-start = ((f32[2,128,160]{2,0,1:T(2,128)}), f32[2,128,160]{2,0,1:T(2,128)S(1)}, u32[]{:S(2)}, u32[]{:S(2)}) async-start(f32[2,128,160]{2,0,1:T(2,128)} %copy.138), calls=%async_computation | async-start | bytes 524288 | tf_op jit(solution)/shard_map/all_to_all | solution.py:105
  57.9 0.5 iota_compare_fusion.5
  58.5 9.4 %all-to-all-done = f32[2,128,160]{2,0,1:T(2,128)S(1)} async-done(((f32[2,128,160]{2,0,1:T(2,128)}), f32[2,128,160]{2,0,1:T(2,128)S(1)}, u32[]{:S(2)}, u32[]{:S(2)}) %all-to-all-start) | async-done | bytes 163872 | tf_op jit(solution)/shard_map/all_to_all | solution.py:105
  67.9 0.1 subtract_convert_fusion
  68.1 0.1 reshape.241
  68.5 1.1 fusion.44
  69.7 2.0 bitcast_reduce_fusion
  71.7 0.7 fusion.8
  72.5 0.9 convolution_bitcast_fusion.1
  73.4 0.1 convert_element_type.86
  73.5 0.2 fusion.10
  73.8 0.7 convert_element_type.89
  74.5 2.0 copy_bitcast_fusion
  76.5 4.3 %all-to-all-start.1 = ((bf16[128,16,128]{2,0,1:T(8,128)(2,1)}), bf16[128,16,128]{2,0,1:T(8,128)(2,1)}, u32[]{:S(2)}, u32[]{:S(2)}) async-start(bf16[128,16,128]{2,0,1:T(8,128)(2,1)} %copy_bitcast_fusion), calls=%async_computation.1 | async-start | bytes 1048576 | tf_op jit(solution)/shard_map/all_to_all | solution.py:138
  80.9 0.5 copy-done.5
  81.5 0.2 reduce_window_sum.11
  81.6 15.3 %all-to-all-done.1 = bf16[128,16,128]{2,0,1:T(8,128)(2,1)} async-done(((bf16[128,16,128]{2,0,1:T(8,128)(2,1)}), bf16[128,16,128]{2,0,1:T(8,128)(2,1)}, u32[]{:S(2)}, u32[]{:S(2)}) %all-to-all-start.1) | async-done | bytes 524320 | tf_op jit(solution)/shard_map/all_to_all | solution.py:138
  97.0 16.4 %all-gather.5.cloned.1.call-done = bf16[2,128,2048]{2,1,0:T(8,128)(2,1)} async-done(((bf16[2,8,2048]{2,1,0:T(8,128)(2,1)}), bf16[2,128,2048]{2,1,0:T(8,128)(2,1)}) %all-gather.5.cloned.1.call-update) | async-done | bytes 1048592 | tf_op jit(solution)/shard_map/all_gather | solution.py:141
  113.4 1.8 fusion.45
  115.1 0.8 copy.161
  115.9 3.6 %all-to-all-start.2 = ((f32[2,128,128]{2,0,1:T(2,128)}), f32[2,128,128]{2,0,1:T(2,128)S(1)}, u32[]{:S(2)}, u32[]{:S(2)}) async-start(f32[2,128,128]{2,0,1:T(2,128)} %copy.161), calls=%async_computation.2 | async-start | bytes 262144 | tf_op jit(solution)/shard_map/all_to_all | solution.py:145
  119.5 0.8 select_reduce_fusion
  120.4 0.5 copy-done.6
  120.8 0.7 multiply_add_fusion.1
  121.5 6.0 %all-to-all-done.2 = f32[2,128,128]{2,0,1:T(2,128)S(1)} async-done(((f32[2,128,128]{2,0,1:T(2,128)}), f32[2,128,128]{2,0,1:T(2,128)S(1)}, u32[]{:S(2)}, u32[]{:S(2)}) %all-to-all-start.2) | async-done | bytes 131104 | tf_op jit(solution)/shard_map/all_to_all | solution.py:145
  127.5 0.1 multiply_reduce_fusion
  127.6 0.8 fusion.28
  128.4 0.4 convolution_convert_fusion
  128.8 27.4 %all_to_all.62 = bf16[16,16,2048]{2,1,0:T(8,128)(2,1)S(1)} all-to-all(bf16[16,16,2048]{2,1,0:T(8,128)(2,1)S(1)} %bitcast.120), channel_id=1, replica_groups=mesh['groups'=2,'ep'=16] {'ep'}, dimensions={0} | all-to-all | bytes 2097152 | tf_op jit(solution)/shard_map/all_to_all | solution.py:167
  156.2 4.6 %fusion = f32[16,16,1536]{2,1,0:T(8,128)S(1)} fusion(bf16[16,16,2048]{2,1,0:T(8,128)(2,1)S(1)} %all_to_all.62, bf16[1,2048,1536]{2,1,0:T(8,128)(2,1)} %param.22), kind=kOutput, calls=%fused_computation.1 | convolution fusion | flops 1610612736 | bytes 8912896 | tf_op jit(solution)/shard_map/nsd,df->nsf/dot_general | solution.py:165
  160.8 2.1 %fusion.4 = bf16[16,16,2048]{2,1,0:T(8,128)(2,1)} fusion(bf16[1,768,2048]{2,1,0:T(8,128)(2,1)S(1)} %copy-done, f32[16,16,1536]{2,1,0:T(8,128)S(1)} %fusion), kind=kOutput, calls=%fused_computation.6 | convolution fusion | flops 807010304 | bytes 5767168 | tf_op jit(solution)/shard_map/nsf,fd->nsd/dot_general | solution.py:173
  162.9 5.1 %all-to-all-start.4 = ((bf16[16,16,2048]{2,1,0:T(8,128)(2,1)}), bf16[16,16,2048]{2,1,0:T(8,128)(2,1)}, u32[]{:S(2)}, u32[]{:S(2)}) async-start(bf16[16,16,2048]{2,1,0:T(8,128)(2,1)} %fusion.4), calls=%async_computation.4 | async-start | bytes 2097152 | tf_op jit(solution)/shard_map/all_to_all | solution.py:176
  168.1 0.1 convert_element_type.98
  168.3 0.6 pad_maximum_fusion.1
  168.9 22.1 %all-to-all-done.4 = bf16[16,16,2048]{2,1,0:T(8,128)(2,1)} async-done(((bf16[16,16,2048]{2,1,0:T(8,128)(2,1)}), bf16[16,16,2048]{2,1,0:T(8,128)(2,1)}, u32[]{:S(2)}, u32[]{:S(2)}) %all-to-all-start.4) | async-done | bytes 1048608 | tf_op jit(solution)/shard_map/all_to_all | solution.py:176
  191.0 3.6 %gather_fusion = bf16[128,2048]{1,0:T(8,128)(2,1)} fusion(bf16[256,2048]{1,0:T(8,128)(2,1)} %bitcast.33, s32[1024]{0:T(1024)S(1)} %pad_clamp_fusion), kind=kCustom, calls=%fused_computation | custom fusion | bytes 1049088 | tf_op jit(solution)/shard_map/gather | solution.py:177
  194.6 1.5 fusion.13
  196.1 0.7 fusion.42
  (61 shorter events, 1.3 us)
Async XLA Ops:
  7.2 153.6 %copy-start = (bf16[1,768,2048]{2,1,0:T(8,128)(2,1)S(1)}, bf16[1,768,2048]{2,1,0:T(8,128)(2,1)}, u32[]{:S(2)}) copy-start(bf16[1,768,2048]{2,1,0:T(8,128)(2,1)} %param.23) | copy-start | bytes 9437188
  7.2 44.3 %all-gather.3.cloned.1.call-start = ((), (), s32[]{:S(2)}) async-start(), calls=%async_computation.5 | async-start | bytes 1114112 | tf_op jit(solution)/shard_map/all_gather | solution.py:101
  13.2 4.4 %copy-start.11 = (s32[8]{0:T(128)S(1)}, s32[8]{0:T(128)}, u32[]{:S(2)}) copy-start(s32[8]{0:T(128)} %param.27) | copy-start | bytes 100
  13.2 4.5 %copy-start.8 = (s32[2]{0:T(128)S(1)}, s32[2]{0:T(128)}, u32[]{:S(2)}) copy-start(s32[2]{0:T(128)} %param.26) | copy-start | bytes 28
  13.2 38.3 %copy-start.9 = (bf16[2048,16]{0,1:T(8,128)(2,1)S(1)}, bf16[2048,16]{0,1:T(8,128)(2,1)}, u32[]{:S(2)}) copy-start(bf16[2048,16]{0,1:T(8,128)(2,1)} %param.20) | copy-start | bytes 196612
  13.2 38.3 %copy-start.10 = (bf16[2048,16]{0,1:T(8,128)(2,1)S(1)}, bf16[2048,16]{0,1:T(8,128)(2,1)}, u32[]{:S(2)}) copy-start(bf16[2048,16]{0,1:T(8,128)(2,1)} %param.19) | copy-start | bytes 196612
  54.2 13.7 %all-to-all-start = ((f32[2,128,160]{2,0,1:T(2,128)}), f32[2,128,160]{2,0,1:T(2,128)S(1)}, u32[]{:S(2)}, u32[]{:S(2)}) async-start(f32[2,128,160]{2,0,1:T(2,128)} %copy.138), calls=%async_computation | async-start | bytes 524288 | tf_op jit(solution)/shard_map/all_to_all | solution.py:105
  57.8 55.5 %all-gather.5.cloned.1.call-start = ((), (), s32[]{:S(2)}) async-start(), calls=%async_computation.6 | async-start | bytes 1114112 | tf_op jit(solution)/shard_map/all_gather | solution.py:141
  69.7 2.8 %copy-start.2 = (bf16[2,1024,2,128]{3,2,1,0:T(2,128)(2,1)S(1)}, bf16[2,1024,2,128]{3,2,1,0:T(2,128)(2,1)}, u32[]{:S(2)}) copy-start(bf16[2,1024,2,128]{3,2,1,0:T(2,128)(2,1)} %reshape.242) | copy-start | bytes 3145732
  73.4 7.4 %copy-start.3 = (s32[8,2,8]{2,1,0:T(2,128)S(1)}, s32[8,2,8]{2,1,0:T(2,128)}, u32[]{:S(2)}) copy-start(s32[8,2,8]{2,1,0:T(2,128)} %param.28) | copy-start | bytes 1540
  74.5 53.0 %copy-start.1 = (f32[2,8,2048]{2,1,0:T(8,128)S(1)}, f32[2,8,2048]{2,1,0:T(8,128)}, u32[]{:S(2)}) copy-start(f32[2,8,2048]{2,1,0:T(8,128)} %param.15) | copy-start | bytes 393220
  76.5 20.5 %all-to-all-start.1 = ((bf16[128,16,128]{2,0,1:T(8,128)(2,1)}), bf16[128,16,128]{2,0,1:T(8,128)(2,1)}, u32[]{:S(2)}, u32[]{:S(2)}) async-start(bf16[128,16,128]{2,0,1:T(8,128)(2,1)} %copy_bitcast_fusion), calls=%async_computation.1 | async-start | bytes 1048576 | tf_op jit(solution)/shard_map/all_to_all | solution.py:138
  80.9 0.5 copy-start.5
  115.9 11.6 %all-to-all-start.2 = ((f32[2,128,128]{2,0,1:T(2,128)}), f32[2,128,128]{2,0,1:T(2,128)S(1)}, u32[]{:S(2)}, u32[]{:S(2)}) async-start(f32[2,128,128]{2,0,1:T(2,128)} %copy.161), calls=%async_computation.2 | async-start | bytes 262144 | tf_op jit(solution)/shard_map/all_to_all | solution.py:145
  120.4 0.5 copy-start.6
  162.9 5.2 %copy-start.7 = (s32[128]{0:T(128)S(1)}, s32[128]{0:T(128)}, u32[]{:S(2)}) copy-start(s32[128]{0:T(128)} %copy-done.6) | copy-start | bytes 1540
  162.9 28.1 %all-to-all-start.4 = ((bf16[16,16,2048]{2,1,0:T(8,128)(2,1)}), bf16[16,16,2048]{2,1,0:T(8,128)(2,1)}, u32[]{:S(2)}, u32[]{:S(2)}) async-start(bf16[16,16,2048]{2,1,0:T(8,128)(2,1)} %fusion.4), calls=%async_computation.4 | async-start | bytes 2097152 | tf_op jit(solution)/shard_map/all_to_all | solution.py:176
  191.0 3.6 %copy-start.4 = (f32[2,8,8]{2,1,0:T(8,128)S(1)}, f32[2,8,8]{2,1,0:T(8,128)}, u32[]{:S(2)}) copy-start(f32[2,8,8]{2,1,0:T(8,128)} %param.29) | copy-start | bytes 1540
Sparse Core Ops, SparseCore 0:
  10.8 40.6 all-gather.2
  74.6 38.7 all-gather.4
where the time goes:
time: 206 us; the launch traced here: 204 us
  waiting for transfers between devices  103 us (50%)
  blocking collectives  27.4 us (13%)
  starting transfers between devices  16.7 us (8%)
  local copies, waits for them, and re-layouts  16.2 us (8%)
  matrix products  15 us (7%)
  between operations  14.4 us (7%)
  other arithmetic  11 us (5%)
    all_gather x1, waiting for transfers between devices, shards(): lax.all_gather(normed, 'ep', axis=1, tiled=True)  33.7 us
    all_to_all x1, blocking collectives, shards(): lax.all_to_all(outgoing, 'ep', split_axis=0, concat_axis=0, tiled=True)  27.4 us
    all_to_all x1, waiting for transfers between devices, shards(): lax.all_to_all(expert_done, 'ep', split_axis=0, concat_axis=0, tiled=True)  22.1 us
    all_gather x1, waiting for transfers between devices, shards(): lax.all_gather(attended, 'ep', axis=1, tiled=True)  16.4 us
    all_to_all x1, waiting for transfers between devices, shards(): lax.all_to_all(w_output, 'ep', split_axis=1, concat_axis=0, tiled=True)  15.3 us
    all_to_all x1, waiting for transfers between devices, shards(): lax.all_to_all(head_parts, 'ep', split_axis=1, concat_axis=2, tiled=True)  9.38 us
    all_to_all x1, waiting for transfers between devices, shards(): lax.all_to_all(column_part, 'ep', split_axis=1, concat_axis=2, tiled=True)  5.96 us
    all_to_all x1, starting transfers between devices, shards(): lax.all_to_all(expert_done, 'ep', split_axis=0, concat_axis=0, tiled=True)  5.1 us
  transfers between devices with their start and end apart: 6, of which 6 were waited for; matrix products, arithmetic and copies ran while one was open for 6% of the time, Pallas kernels for 0%

commit v1 on v0

--- a/solution.py
+++ b/solution.py
@@ -3,6 +3,8 @@
 import jax
 import jax.numpy as jnp
 from jax import lax
+from jax.experimental import pallas as pl
+from jax.experimental.pallas import tpu as pltpu
 from jax.sharding import PartitionSpec as P
 
 HQ = 16
@@ -187,9 +189,520 @@
     return (hidden + mixture, appended)
 
 
+TUNED_DEVICES = 16
+ROWS = 16
+
+
+def norm_rows(values, gain):
+    squares = jnp.mean(values * values, axis=-1, keepdims=True)
+    return values * lax.rsqrt(squares + EPS) * gain
+
+
+def layer_kernel(
+    states,
+    attn_gain,
+    moe_gain,
+    w_query,
+    w_key,
+    w_value,
+    aux,
+    gates,
+    w_output,
+    w_gate_up,
+    w_down,
+    key_cache,
+    value_cache,
+    out,
+    appended,
+    w_joined,
+    gather_q,
+    gather_o,
+    gather_m,
+    parts,
+    own_parts,
+    w_cols,
+    cols,
+    own_cols,
+    hidden,
+    act,
+    expert_out,
+    returned,
+    fresh_k,
+    fresh_v,
+    queries,
+    gate_up_v,
+    down_v,
+    keys_v,
+    values_v,
+    load_sem,
+    ag_send,
+    ag_recv,
+    a2a_send,
+    a2a_recv,
+):
+    n = TUNED_DEVICES
+    half = n // 2
+    me = lax.axis_index("ep")
+    c = me % 2
+    y = (me // 2) % 2
+    z = me // 4
+    near = me // half
+    z_other = (z, z + 1 - 2 * (z % 2), (z + 2) % 4, 3 - z)
+
+    def index_of(zz, yy, cc):
+        return (zz * 2 + yy) * 2 + cc
+
+    def block(ref, i, rows=ROWS):
+        return ref.at[pl.ds(pl.multiple_of(i * rows, rows), rows), :]
+
+    def rdma(src, dst, send, recv, target):
+        return pltpu.make_async_remote_copy(
+            src_ref=src,
+            dst_ref=dst,
+            send_sem=send,
+            recv_sem=recv,
+            device_id={"ep": target},
+            device_id_type=pl.DeviceIdType.MESH,
+        )
+
+    barrier = pltpu.get_barrier_semaphore()
+    for i in range(1, n):
+        pl.semaphore_signal(
+            barrier,
+            inc=1,
+            device_id={"ep": (me + i) % n},
+            device_id_type=pl.DeviceIdType.MESH,
+        )
+
+    loads = [
+        pltpu.make_async_copy(key_cache, keys_v, load_sem.at[0]),
+        pltpu.make_async_copy(value_cache, values_v, load_sem.at[1]),
+        pltpu.make_async_copy(w_gate_up, gate_up_v, load_sem.at[2]),
+        pltpu.make_async_copy(w_down, down_v, load_sem.at[3]),
+        pltpu.make_async_copy(
+            w_output.at[:, pl.ds(pl.multiple_of(me * 128, 128), 128)],
+            block(w_cols, me, 128),
+            load_sem.at[4],
+        ),
+    ]
+    for load in loads:
+        load.start()
+
+    class Gather:
+        def __init__(self, buf, phase):
+            self.buf, self.phase, self.sends = buf, phase, []
+
+        def push(self, src, target):
+            k = len(self.sends)
+            copy = rdma(
+                block(self.buf, src),
+                block(self.buf, src),
+                ag_send.at[self.phase, k],
+                ag_recv.at[self.phase, src],
+                target,
+            )
+            copy.start()
+            self.sends.append(copy)
+
+        def arrived(self, src):
+            rdma(
+                block(self.buf, src),
+                block(self.buf, src),
+                ag_send.at[self.phase, 0],
+                ag_recv.at[self.phase, src],
+                index_of(z, y, 1 - c),
+            ).wait_recv()
+
+        def begin(self):
+            for i in (2, 3, 1):
+                self.push(me, index_of(z_other[i], y, c))
+            self.push(me, index_of(z, 1 - y, c))
+            self.push(me, index_of(z, y, 1 - c))
+
+        def from_z(self, i):
+            src = index_of(z_other[i], y, c)
+            self.arrived(src)
+            self.push(src, index_of(z, 1 - y, c))
+            self.push(src, index_of(z, y, 1 - c))
+
+        def from_y(self, i):
+            src = index_of(z_other[i], 1 - y, c)
+            self.arrived(src)
+            self.push(src, index_of(z, y, 1 - c))
+
+        def from_core(self, i):
+            self.arrived(index_of(z_other[i], y, 1 - c))
+            self.arrived(index_of(z_other[i], 1 - y, 1 - c))
+
+        def near_ready(self):
+            self.from_y(0)
+            self.from_z(1)
+            self.from_y(1)
+            self.from_core(0)
+            self.from_core(1)
+
+        def far_forward(self):
+            self.from_z(2)
+            self.from_z(3)
+
+        def far_ready(self):
+            self.from_y(2)
+            self.from_y(3)
+            self.from_core(2)
+            self.from_core(3)
+
+        def finish(self):
+            for copy in self.sends:
+                copy.wait_send()
+
+    def scatter(src, dst, phase, group, is_near):
+        first = 1 if is_near else 0
+        for i in range(first, half):
+            p = group * half + (me + i) % half
+            rdma(
+                block(src, p),
+                block(dst, me),
+                a2a_send.at[phase, p],
+                a2a_recv.at[phase, me],
+                p,
+            ).start()
+        if is_near:
+            block(dst, me)[...] = block(src, me)[...]
+
+    def scatter_wait(src, dst, phase, rows=ROWS):
+        for i in range(1, n):
+            p = (me + i) % n
+            rdma(
+                block(src, p, rows),
+                block(dst, p, rows),
+                a2a_send.at[phase, p],
+                a2a_recv.at[phase, p],
+                p,
+            ).wait_recv()
+
+    def scatter_sent(src, dst, phase):
+        for i in range(1, n):
+            p = (me + i) % n
+            rdma(
+                block(src, p),
+                block(dst, p),
+                a2a_send.at[phase, p],
+                a2a_recv.at[phase, p],
+                p,
+            ).wait_send()
+
+    def w_copy(p, landing):
+        return rdma(
+            w_output.at[:, pl.ds(pl.multiple_of(p * 128, 128), 128)],
+            block(w_cols, landing, 128),
+            a2a_send.at[3, p],
+            a2a_recv.at[3, landing],
+            p,
+        )
+
+    block(gather_q, me)[...] = norm_rows(states[...], attn_gain[...]).astype(jnp.bfloat16)
+    pl.semaphore_wait(barrier, n - 1)
+
+    first = Gather(gather_q, 0)
+    first.begin()
+    w_joined[:, 0:128] = w_query[...]
+    w_joined[:, 128:144] = w_key[...]
+    w_joined[:, 144:160] = w_value[...]
+    w_joined[:, 160:256] = jnp.zeros((w_joined.shape[0], 96), jnp.bfloat16)
+
+    def group_rows(group):
+        return pl.ds(pl.multiple_of(group * 128, 128), 128)
+
+    first.near_ready()
+    parts[group_rows(near), :] = jnp.dot(
+        gather_q[group_rows(near), :], w_joined[...], preferred_element_type=jnp.float32
+    )
+    scatter(parts, own_parts, 0, near, True)
+    first.far_forward()
+    first.far_ready()
+    parts[group_rows(1 - near), :] = jnp.dot(
+        gather_q[group_rows(1 - near), :], w_joined[...], preferred_element_type=jnp.float32
+    )
+    scatter(parts, own_parts, 0, 1 - near, False)
+    for i in range(1, n):
+        w_copy((me + i) % n, me).start()
+    first.finish()
+    scatter_wait(parts, own_parts, 0)
+
+    cosine = aux[:, 0:128]
+    sine = aux[:, 128:256]
+
+    def turned(vectors):
+        return vectors * cosine + pltpu.roll(vectors, 64, 1) * sine
+
+    for j in range(n):
+        rows = slice(j * ROWS, (j + 1) * ROWS)
+        queries[rows, :] = turned(own_parts[rows, 0:128]).astype(jnp.bfloat16)
+        fresh_k[:, j * 16 : (j + 1) * 16] = own_parts[rows, 128:144]
+        fresh_v[:, j * 16 : (j + 1) * 16] = own_parts[rows, 144:160]
+    loads[0].wait()
+    loads[1].wait()
+    inv_root = 1.0 / math.sqrt(HD)
+    group_size = HQ // KVH
+    q_rows = group_size * ROWS
+    span = keys_v.shape[1]
+    far_pos = lax.broadcasted_iota(jnp.int32, (q_rows, span), 1).astype(jnp.float32)
+    row_at = lax.broadcasted_iota(jnp.int32, (q_rows, ROWS), 0) % ROWS
+    col_at = lax.broadcasted_iota(jnp.int32, (q_rows, ROWS), 1)
+    own_seen = (row_at % 8 == col_at % 8) & (col_at // 8 <= row_at // 8)
+    limits = [jnp.concatenate([aux[:, 256 + p : 257 + p]] * group_size, axis=0) for p in range(2)]
+    for k in range(KVH):
+        lanes = slice(k * HD, (k + 1) * HD)
+        new_keys = turned(fresh_k[:, lanes]).astype(jnp.bfloat16)
+        new_values = fresh_v[:, lanes].astype(jnp.bfloat16)
+        appended[:, lanes] = new_keys
+        appended[:, slice((KVH + k) * HD, (KVH + k + 1) * HD)] = new_values
+        q = queries[k * q_rows : (k + 1) * q_rows, :]
+
+        def against(rows):
+            return (
+                lax.dot_general(
+                    q, rows, (((1,), (1,)), ((), ())), preferred_element_type=jnp.float32
+                )
+                * inv_root
+            )
+
+        scores = [
+            jnp.where(far_pos < limits[p], against(keys_v[p, :, lanes]), -1e30) for p in range(2)
+        ]
+        own_scores = jnp.where(own_seen, against(new_keys), -1e30)
+        peak = jnp.maximum(
+            jnp.maximum(
+                jnp.max(scores[0], axis=1, keepdims=True), jnp.max(scores[1], axis=1, keepdims=True)
+            ),
+            jnp.max(own_scores, axis=1, keepdims=True),
+        )
+        weights = [jnp.exp(s - peak) for s in scores]
+        own_weights = jnp.exp(own_scores - peak)
+        total = (
+            jnp.sum(weights[0], axis=1, keepdims=True)
+            + jnp.sum(weights[1], axis=1, keepdims=True)
+            + jnp.sum(own_weights, axis=1, keepdims=True)
+        )
+        scale = 1.0 / total
+        attended = jnp.dot(
+            (own_weights * scale).astype(jnp.bfloat16),
+            new_values,
+            preferred_element_type=jnp.float32,
+        )
+        for p in range(2):
+            attended = attended + jnp.dot(
+                (weights[p] * scale).astype(jnp.bfloat16),
+                values_v[p, :, lanes],
+                preferred_element_type=jnp.float32,
+            )
+        attended = attended.astype(jnp.bfloat16)
+        for g in range(group_size):
+            h = k * group_size + g
+            gather_o[pl.ds(pl.multiple_of(me * ROWS, ROWS), ROWS), h * HD : (h + 1) * HD] = (
+                attended[g * ROWS : (g + 1) * ROWS, :]
+            )
+
+    second = Gather(gather_o, 1)
+    second.begin()
+    scatter_sent(parts, own_parts, 0)
+    loads[4].wait()
+    for i in range(1, n):
+        w_copy((me + i) % n, (me + i) % n).wait_recv()
+    second.near_ready()
+    cols[group_rows(near), :] = jnp.dot(
+        gather_o[group_rows(near), :], w_cols[...], preferred_element_type=jnp.float32
+    )
+    scatter(cols, own_cols, 1, near, True)
+    second.far_forward()
+    second.far_ready()
+    cols[group_rows(1 - near), :] = jnp.dot(
+        gather_o[group_rows(1 - near), :], w_cols[...], preferred_element_type=jnp.float32
+    )
+    scatter(cols, own_cols, 1, 1 - near, False)
+    second.finish()
+    for i in range(1, n):
+        w_copy((me + i) % n, (me + i) % n).wait_send()
+    scatter_wait(cols, own_cols, 1)
+    for j in range(n):
+        lanes = slice(j * 128, (j + 1) * 128)
+        hidden[:, lanes] = states[:, lanes] + own_cols[j * ROWS : (j + 1) * ROWS, :]
+    block(gather_m, me)[...] = norm_rows(hidden[...], moe_gain[...]).astype(jnp.bfloat16)
+
+    third = Gather(gather_m, 2)
+    third.begin()
+    scatter_sent(cols, own_cols, 1)
+    loads[2].wait()
+    loads[3].wait()
+    ff = down_v.shape[0]
+
+    def gate_up(group):
+        @pl.loop(0, ff // 256)
+        def _(t):
+            at = pl.multiple_of(t * 256, 256)
+            inputs = gather_m[group_rows(group), :]
+            g = jnp.dot(
+                inputs, gate_up_v[:, pl.ds(at, 256)], preferred_element_type=jnp.float32
+            )
+            u = jnp.dot(
+                inputs,
+                gate_up_v[:, pl.ds(pl.multiple_of(ff + t * 256, 256), 256)],
+                preferred_element_type=jnp.float32,
+            )
+            act[:, pl.ds(at, 256)] = (g / (1.0 + jnp.exp(-g)) * u).astype(jnp.bfloat16)
+
+    def down(group):
+        @pl.loop(0, down_v.shape[1] // 512)
+        def _(t):
+            at = pl.multiple_of(t * 512, 512)
+            expert_out[group_rows(group), pl.ds(at, 512)] = jnp.dot(
+                act[...], down_v[:, pl.ds(at, 512)], preferred_element_type=jnp.float32
+            ).astype(jnp.bfloat16)
+
+    third.near_ready()
+    gate_up(near)
+    third.far_forward()
+    down(near)
+    scatter(expert_out, returned, 2, near, True)
+    third.far_ready()
+    gate_up(1 - near)
+    down(1 - near)
+    scatter(expert_out, returned, 2, 1 - near, False)
+    third.finish()
+
+    lane_at = lax.broadcasted_iota(jnp.int32, gates.shape, 1)
+
+    def mixed(total, e):
+        gate = jnp.sum(jnp.where(lane_at == e, gates[...], 0.0), axis=1, keepdims=True)
+        got = block(returned, e)[...].astype(jnp.float32)
+        return total + jnp.where(gate > 0.0, gate * got, 0.0)
+
+    total = mixed(hidden[...], me)
+    for group, start in ((near, 1), (1 - near, 0)):
+        for i in range(start, half):
+            e = group * half + (me + i) % half
+            rdma(
+                block(expert_out, e),
+                block(returned, e),
+                a2a_send.at[2, e],
+                a2a_recv.at[2, e],
+                e,
+            ).wait_recv()
+            total = mixed(total, e)
+    out[...] = total
+    scatter_sent(expert_out, returned, 2)
+
+
+def tuned(
+    states,
+    attn_gain,
+    moe_gain,
+    w_query,
+    w_key,
+    w_value,
+    w_output,
+    w_gate_up,
+    w_down,
+    key_cache,
+    value_cache,
+    cache_lengths,
+    prefix_slot,
+    routes,
+    gate_weights,
+):
+    n = lax.axis_size("ep")
+    step_count, row_count, width = states.shape
+    rows = step_count * row_count
+    prefix_count, span, kv_width = key_cache.shape
+    ff = w_down.shape[1]
+    mine = prefix_slot[:, None] == jnp.arange(prefix_count)[None, :]
+    limits = jnp.where(mine, cache_lengths[None, :], 0)
+    positions = (
+        jnp.sum(limits, axis=1).astype(jnp.float32)[None, :]
+        + jnp.arange(step_count).astype(jnp.float32)[:, None]
+    ).reshape(rows, 1)
+    inverse_rate = THETA ** (-(jnp.arange(HD // 2).astype(jnp.float32) * 2.0 / HD))
+    phases = positions * inverse_rate[None, :]
+    cosine, sine = jnp.cos(phases), jnp.sin(phases)
+    limits = jnp.tile(limits.astype(jnp.float32), (step_count, 1))
+    aux = jnp.concatenate(
+        [cosine, cosine, -sine, sine, jnp.pad(limits, ((0, 0), (0, 128 - prefix_count)))], axis=1
+    )
+    chosen = jnp.swapaxes(routes, 0, 1).reshape(rows, TOPK)
+    gates = jnp.sum(
+        jnp.where(
+            chosen[:, :, None] == jnp.arange(128)[None, None, :],
+            gate_weights.reshape(rows, TOPK)[:, :, None],
+            0.0,
+        ),
+        axis=1,
+    )
+    in_vmem = pl.BlockSpec(memory_space=pltpu.VMEM)
+    in_hbm = pl.BlockSpec(memory_space=pl.ANY)
+    everyone = n * rows
+    bf16, f32 = jnp.bfloat16, jnp.float32
+    out, appended = pl.pallas_call(
+        layer_kernel,
+        out_shape=(
+            jax.ShapeDtypeStruct((rows, width), f32),
+            jax.ShapeDtypeStruct((rows, 2 * kv_width), bf16),
+        ),
+        in_specs=[in_vmem] * 8 + [in_hbm] * 5,
+        out_specs=(in_vmem, in_vmem),
+        scratch_shapes=[
+            pltpu.VMEM((width, 256), bf16),
+            pltpu.VMEM((everyone, width), bf16),
+            pltpu.VMEM((everyone, width), bf16),
+            pltpu.VMEM((everyone, width), bf16),
+            pltpu.VMEM((everyone, 256), f32),
+            pltpu.VMEM((everyone, 256), f32),
+            pltpu.VMEM((width, 128), bf16),
+            pltpu.VMEM((everyone, 128), f32),
+            pltpu.VMEM((everyone, 128), f32),
+            pltpu.VMEM((rows, width), f32),
+            pltpu.VMEM((everyone // 2, ff), bf16),
+            pltpu.VMEM((everyone, width), bf16),
+            pltpu.VMEM((everyone, width), bf16),
+            pltpu.VMEM((rows, kv_width), f32),
+            pltpu.VMEM((rows, kv_width), f32),
+            pltpu.VMEM((HQ * rows, HD), bf16),
+            pltpu.VMEM((width, 2 * ff), bf16),
+            pltpu.VMEM((ff, width), bf16),
+            pltpu.VMEM((prefix_count, span, kv_width), bf16),
+            pltpu.VMEM((prefix_count, span, kv_width), bf16),
+            pltpu.SemaphoreType.DMA((5,)),
+            pltpu.SemaphoreType.DMA((3, 16)),
+            pltpu.SemaphoreType.DMA((3, 16)),
+            pltpu.SemaphoreType.DMA((4, 16)),
+            pltpu.SemaphoreType.DMA((4, 16)),
+        ],
+        compiler_params=pltpu.CompilerParams(
+            collective_id=0, has_side_effects=True, vmem_limit_bytes=56 * 1024 * 1024
+        ),
+    )(
+        states.reshape(rows, width),
+        attn_gain.reshape(1, width),
+        moe_gain.reshape(1, width),
+        w_query,
+        w_key,
+        w_value,
+        aux,
+        gates,
+        w_output,
+        w_gate_up[0],
+        w_down[0],
+        key_cache,
+        value_cache,
+    )
+    return (
+        out.reshape(step_count, row_count, width),
+        appended.reshape(step_count, row_count, 2 * kv_width),
+    )
+
+
 def solution(mesh):
     return jax.shard_map(
-        shards,
+        tuned if mesh.shape["ep"] == TUNED_DEVICES else shards,
         mesh=mesh,
         in_specs=(
             P(None, ("groups", "ep"), None),

time: 206 us -> 121 us (0.59)
  the two profiles are of different devices: /device:TPU:0 before, /device:TPU:23 now
where the time goes in v1:
time: 121 us; the launch traced here: 120 us
  Pallas kernels  109 us (90%)
  local copies, waits for them, and re-layouts  8.14 us (7%)
  other arithmetic  2.37 us (2%)
    pallas_call x1, Pallas kernels, tuned(): pl.pallas_call(layer_kernel, out_shape=(jax.ShapeDtypeStruct((rows, width...  109 us
    unnamed x5, local copies, waits for them, and re-layouts  6.67 us

profile of v1, /device:TPU:23, one launch (start us, length us, event | category | flops | bytes accessed | tf_op | source)
XLA Modules:
  0.0 120.2 jit_solution(2066536065775163778)
XLA Ops:
  0.7 0.8 fusion.1
  1.4 0.1 broadcast_add_fusion
  1.5 0.1 add.25
  1.6 0.1 copy.35
  1.7 0.7 copy.37
  2.4 1.4 %select_reduce_fusion.gates = f32[16,128]{1,0:T(8,128)} fusion(f32[16,8]{1,0:T(8,128)} %bitcast.20, s32[16,8]{1,0:T(8,128)S(1)} %bitcast.18), kind=kLoop, calls=%fused_computation | loop fusion | flops 47104 | bytes 9216 | tf_op jit(solution)/shard_map/reduce_sum | solution.py:632
  3.8 0.1 multiply_sine_fusion
  3.9 0.7 concatenate.3.aux
  4.6 1.8 %copy.29.w_key = bf16[2048,16]{1,0:T(8,128)(2,1)} copy(bf16[2048,16]{0,1:T(8,128)(2,1)} %param.19) | data formatting | bytes 131072 | tf_op args[4]
  6.4 1.9 %copy.30.w_value = bf16[2048,16]{1,0:T(8,128)(2,1)} copy(bf16[2048,16]{0,1:T(8,128)(2,1)} %param.20) | data formatting | bytes 131072 | tf_op args[5]
  8.3 109.0 %shard_map.158 = (f32[16,2048]{1,0:T(8,128)}, bf16[16,512]{1,0:T(8,128)(2,1)}) custom-call(f32[16,2048]{1,0:T(8,128)} %bitcast.16, f32[1,2048]{1,0:T(1,128)} %bitcast.22, f32[1,2048]{1,0:T(1,128)} %bitcast.23, bf16[2048,128]{1,0:T(8,128)(2,1)} %w_query.1, bf16[2048,16]{1,0:T(8,128)(2,1)} %copy.29.w_key, bf16[2048,16]{1,0:T(8,128)(2,1)} %copy.30.w_value, ...), custom_call_target="tpu_custom_call" | custom-call | tf_op jit(solution)/shard_map/pallas_call | solution.py:644
  117.3 1.6 %copy.40 = f32[2,8,2048]{2,1,0:T(8,128)} copy(f32[2,8,2048]{2,1,0:T(8,128)} %bitcast.17) | data formatting | bytes 262144
  118.9 1.3 %copy.41 = bf16[2,8,512]{2,1,0:T(8,128)(2,1)} copy(bf16[2,8,512]{2,1,0:T(8,128)(2,1)} %bitcast.19) | data formatting | bytes 32768
  (5 shorter events, 0.0 us)

commit v2 on v1

--- a/solution.py
+++ b/solution.py
@@ -202,11 +202,14 @@
     states,
     attn_gain,
     moe_gain,
+    rates,
+    lengths,
+    slots,
+    routes,
+    gate_weights,
     w_query,
     w_key,
     w_value,
-    aux,
-    gates,
     w_output,
     w_gate_up,
     w_down,
@@ -214,7 +217,13 @@
     value_cache,
     out,
     appended,
-    w_joined,
+    w_query_v,
+    w_kv_v,
+    gates,
+    mirror_gates,
+    relay,
+    summed,
+    from_mirror,
     gather_q,
     gather_o,
     gather_m,
@@ -247,12 +256,15 @@
     y = (me // 2) % 2
     z = me // 4
     near = me // half
-    z_other = (z, z + 1 - 2 * (z % 2), (z + 2) % 4, 3 - z)
+    z_pair = z + 1 - 2 * (z % 2)
+    mirror = (me + half) % n
 
     def index_of(zz, yy, cc):
         return (zz * 2 + yy) * 2 + cc
 
     def block(ref, i, rows=ROWS):
+        if len(ref.shape) == 3:
+            return ref.at[i]
         return ref.at[pl.ds(pl.multiple_of(i * rows, rows), rows), :]
 
     def rdma(src, dst, send, recv, target):
@@ -284,9 +296,12 @@
             block(w_cols, me, 128),
             load_sem.at[4],
         ),
+        pltpu.make_async_copy(w_query, w_query_v, load_sem.at[5]),
+        pltpu.make_async_copy(w_key, w_kv_v.at[0:16, :], load_sem.at[6]),
+        pltpu.make_async_copy(w_value, w_kv_v.at[16:32, :], load_sem.at[7]),
     ]
-    for load in loads:
-        load.start()
+    for i in (5, 6, 7, 0, 1, 4, 2, 3):
+        loads[i].start()
 
     class Gather:
         def __init__(self, buf, phase):
@@ -313,43 +328,36 @@
                 index_of(z, y, 1 - c),
             ).wait_recv()
 
+        def spread(self, src):
+            self.push(src, index_of(z, 1 - y, c))
+            self.push(src, index_of(z_pair, y, c))
+            self.push(src, index_of(z, y, 1 - c))
+
         def begin(self):
-            for i in (2, 3, 1):
-                self.push(me, index_of(z_other[i], y, c))
-            self.push(me, index_of(z, 1 - y, c))
-            self.push(me, index_of(z, y, 1 - c))
-
-        def from_z(self, i):
-            src = index_of(z_other[i], y, c)
+            self.push(me, mirror)
+            self.spread(me)
+
+        def from_y(self, zz, shift):
+            src = (index_of(zz, 1 - y, c) + shift) % n
+            self.arrived(src)
+            self.push(src, index_of(z, y, 1 - c))
+
+        def from_z(self, shift):
+            src = (index_of(z_pair, y, c) + shift) % n
             self.arrived(src)
             self.push(src, index_of(z, 1 - y, c))
             self.push(src, index_of(z, y, 1 - c))
 
-        def from_y(self, i):
-            src = index_of(z_other[i], 1 - y, c)
-            self.arrived(src)
-            self.push(src, index_of(z, y, 1 - c))
-
-        def from_core(self, i):
-            self.arrived(index_of(z_other[i], y, 1 - c))
-            self.arrived(index_of(z_other[i], 1 - y, 1 - c))
-
-        def near_ready(self):
-            self.from_y(0)
-            self.from_z(1)
-            self.from_y(1)
-            self.from_core(0)
-            self.from_core(1)
-
-        def far_forward(self):
-            self.from_z(2)
-            self.from_z(3)
-
-        def far_ready(self):
-            self.from_y(2)
-            self.from_y(3)
-            self.from_core(2)
-            self.from_core(3)
+        def ready(self, shift):
+            self.from_z(shift)
+            self.from_y(z, shift)
+            if shift == 0:
+                self.arrived(mirror)
+                self.spread(mirror)
+            self.from_y(z_pair, shift)
+            for zz in (z, z_pair):
+                for yy in (y, 1 - y):
+                    self.arrived((index_of(zz, yy, 1 - c) + shift) % n)
 
         def finish(self):
             for copy in self.sends:
@@ -405,52 +413,75 @@
 
     first = Gather(gather_q, 0)
     first.begin()
-    w_joined[:, 0:128] = w_query[...]
-    w_joined[:, 128:144] = w_key[...]
-    w_joined[:, 144:160] = w_value[...]
-    w_joined[:, 160:256] = jnp.zeros((w_joined.shape[0], 96), jnp.bfloat16)
+    row_id = lax.broadcasted_iota(jnp.int32, (ROWS, 128), 0)
+    lane_id = lax.broadcasted_iota(jnp.int32, (ROWS, 128), 1)
+    chosen = jnp.concatenate([routes[:, 0, :], routes[:, 1, :]], axis=0)
+    shares = jnp.concatenate([gate_weights[0], gate_weights[1]], axis=0)
+    weighed = jnp.zeros((ROWS, 128), jnp.float32)
+    for k in range(TOPK):
+        weighed = jnp.where(lane_id == chosen[:, k : k + 1], shares[:, k : k + 1], weighed)
+    gates[...] = weighed
+    gates_copy = rdma(gates, mirror_gates, a2a_send.at[5, 1], a2a_recv.at[5, 1], mirror)
+    gates_copy.start()
+    slot_of = jnp.zeros((ROWS, 128), jnp.int32)
+    for b in range(8):
+        slot_of = jnp.where(row_id % 8 == b, slots[b], slot_of)
+    limits = [jnp.where(slot_of == p, lengths[p], 0) for p in range(2)]
+    phases = (limits[0] + limits[1] + row_id // 8).astype(jnp.float32) * rates[...]
+    cosine = jnp.cos(phases)
+    sine = jnp.sin(phases)
+    sine = jnp.where(lane_id < 64, -sine, sine)
 
     def group_rows(group):
         return pl.ds(pl.multiple_of(group * 128, 128), 128)
 
-    first.near_ready()
-    parts[group_rows(near), :] = jnp.dot(
-        gather_q[group_rows(near), :], w_joined[...], preferred_element_type=jnp.float32
-    )
+    first.ready(0)
+    for i in (5, 6, 7):
+        loads[i].wait()
+
+    def project(group):
+        inputs = gather_q[group_rows(group), :]
+        q = jnp.dot(inputs, w_query_v[...], preferred_element_type=jnp.float32)
+        kv = lax.dot_general(
+            inputs, w_kv_v[...], (((1,), (1,)), ((), ())), preferred_element_type=jnp.float32
+        )
+        kv = kv.reshape(half, ROWS, 32)
+        kv = jnp.concatenate([kv[:, 4 * a : 4 * a + 4, :] for a in range(4)], axis=-1)
+        parts[pl.ds(group * half, half), 0:ROWS, :] = q.reshape(half, ROWS, 128)
+        parts[pl.ds(group * half, half), ROWS : ROWS + 4, :] = kv
+        parts[pl.ds(group * half, half), ROWS + 4 : ROWS + 8, :] = jnp.zeros_like(kv)
+
+    project(near)
     scatter(parts, own_parts, 0, near, True)
-    first.far_forward()
-    first.far_ready()
-    parts[group_rows(1 - near), :] = jnp.dot(
-        gather_q[group_rows(1 - near), :], w_joined[...], preferred_element_type=jnp.float32
-    )
+    first.ready(half)
+    project(1 - near)
     scatter(parts, own_parts, 0, 1 - near, False)
     for i in range(1, n):
         w_copy((me + i) % n, me).start()
     first.finish()
     scatter_wait(parts, own_parts, 0)
 
-    cosine = aux[:, 0:128]
-    sine = aux[:, 128:256]
-
     def turned(vectors):
         return vectors * cosine + pltpu.roll(vectors, 64, 1) * sine
 
     for j in range(n):
         rows = slice(j * ROWS, (j + 1) * ROWS)
-        queries[rows, :] = turned(own_parts[rows, 0:128]).astype(jnp.bfloat16)
-        fresh_k[:, j * 16 : (j + 1) * 16] = own_parts[rows, 128:144]
-        fresh_v[:, j * 16 : (j + 1) * 16] = own_parts[rows, 144:160]
+        queries[rows, :] = turned(own_parts[j, 0:ROWS, :]).astype(jnp.bfloat16)
+        packed = own_parts[j, ROWS : ROWS + 4, :]
+        unpacked = jnp.concatenate([packed[:, 32 * a : 32 * a + 32] for a in range(4)], axis=0)
+        fresh_k[:, j * 16 : (j + 1) * 16] = unpacked[:, 0:16]
+        fresh_v[:, j * 16 : (j + 1) * 16] = unpacked[:, 16:32]
     loads[0].wait()
     loads[1].wait()
     inv_root = 1.0 / math.sqrt(HD)
     group_size = HQ // KVH
     q_rows = group_size * ROWS
     span = keys_v.shape[1]
-    far_pos = lax.broadcasted_iota(jnp.int32, (q_rows, span), 1).astype(jnp.float32)
+    far_pos = lax.broadcasted_iota(jnp.int32, (q_rows, span), 1)
     row_at = lax.broadcasted_iota(jnp.int32, (q_rows, ROWS), 0) % ROWS
     col_at = lax.broadcasted_iota(jnp.int32, (q_rows, ROWS), 1)
     own_seen = (row_at % 8 == col_at % 8) & (col_at // 8 <= row_at // 8)
-    limits = [jnp.concatenate([aux[:, 256 + p : 257 + p]] * group_size, axis=0) for p in range(2)]
+    limits = [jnp.concatenate([m[:, 0:1]] * group_size, axis=0) for m in limits]
     for k in range(KVH):
         lanes = slice(k * HD, (k + 1) * HD)
         new_keys = turned(fresh_k[:, lanes]).astype(jnp.bfloat16)
@@ -509,13 +540,12 @@
     loads[4].wait()
     for i in range(1, n):
         w_copy((me + i) % n, (me + i) % n).wait_recv()
-    second.near_ready()
+    second.ready(0)
     cols[group_rows(near), :] = jnp.dot(
         gather_o[group_rows(near), :], w_cols[...], preferred_element_type=jnp.float32
     )
     scatter(cols, own_cols, 1, near, True)
-    second.far_forward()
-    second.far_ready()
+    second.ready(half)
     cols[group_rows(1 - near), :] = jnp.dot(
         gather_o[group_rows(1 - near), :], w_cols[...], preferred_element_type=jnp.float32
     )
@@ -559,38 +589,68 @@
                 act[...], down_v[:, pl.ds(at, 512)], preferred_element_type=jnp.float32
             ).astype(jnp.bfloat16)
 
-    third.near_ready()
+    third.ready(0)
     gate_up(near)
-    third.far_forward()
     down(near)
-    scatter(expert_out, returned, 2, near, True)
-    third.far_ready()
+    for i in range(1, half):
+        mate = near * half + (me + i) % half
+        rdma(
+            block(expert_out, mate),
+            block(returned, me % half),
+            a2a_send.at[2, mate],
+            a2a_recv.at[2, me],
+            mate,
+        ).start()
+    third.ready(half)
     gate_up(1 - near)
     down(1 - near)
-    scatter(expert_out, returned, 2, 1 - near, False)
+    for i in range(1, half):
+        mate = near * half + (me + i) % half
+        rdma(
+            block(expert_out, (mate + half) % n),
+            block(relay, me % half),
+            a2a_send.at[4, mate],
+            a2a_recv.at[4, me],
+            mate,
+        ).start()
     third.finish()
 
-    lane_at = lax.broadcasted_iota(jnp.int32, gates.shape, 1)
-
-    def mixed(total, e):
-        gate = jnp.sum(jnp.where(lane_at == e, gates[...], 0.0), axis=1, keepdims=True)
-        got = block(returned, e)[...].astype(jnp.float32)
-        return total + jnp.where(gate > 0.0, gate * got, 0.0)
-
-    total = mixed(hidden[...], me)
-    for group, start in ((near, 1), (1 - near, 0)):
-        for i in range(start, half):
-            e = group * half + (me + i) % half
+    def mixed(total, shares, e, got):
+        share = jnp.sum(jnp.where(lane_id == e, shares[...], 0.0), axis=1, keepdims=True)
+        return total + jnp.where(share > 0.0, share * got[...].astype(jnp.float32), 0.0)
+
+    def mix(total, shares, phase, buf):
+        for i in range(1, half):
+            e = near * half + (me + i) % half
             rdma(
                 block(expert_out, e),
-                block(returned, e),
-                a2a_send.at[2, e],
-                a2a_recv.at[2, e],
+                block(buf, e % half),
+                a2a_send.at[phase, e],
+                a2a_recv.at[phase, e],
                 e,
             ).wait_recv()
-            total = mixed(total, e)
-    out[...] = total
-    scatter_sent(expert_out, returned, 2)
+            total = mixed(total, shares, e, block(buf, e % half))
+        return total
+
+    gates_copy.wait()
+    total = mixed(jnp.zeros(hidden.shape, jnp.float32), mirror_gates, me, block(expert_out, mirror))
+    summed[...] = mix(total, mirror_gates, 4, relay)
+    sum_copy = rdma(summed, from_mirror, a2a_send.at[5, 0], a2a_recv.at[5, 0], mirror)
+    sum_copy.start()
+    total = mixed(hidden[...], gates, me, block(expert_out, me))
+    total = mix(total, gates, 2, returned)
+    sum_copy.wait()
+    out[...] = total + from_mirror[...]
+    for phase, buf in ((2, returned), (4, relay)):
+        for i in range(1, half):
+            e = near * half + (me + i) % half
+            rdma(
+                block(expert_out, e),
+                block(buf, e % half),
+                a2a_send.at[phase, e],
+                a2a_recv.at[phase, e],
+                e,
+            ).wait_send()
 
 
 def tuned(
@@ -615,29 +675,10 @@
     rows = step_count * row_count
     prefix_count, span, kv_width = key_cache.shape
     ff = w_down.shape[1]
-    mine = prefix_slot[:, None] == jnp.arange(prefix_count)[None, :]
-    limits = jnp.where(mine, cache_lengths[None, :], 0)
-    positions = (
-        jnp.sum(limits, axis=1).astype(jnp.float32)[None, :]
-        + jnp.arange(step_count).astype(jnp.float32)[:, None]
-    ).reshape(rows, 1)
     inverse_rate = THETA ** (-(jnp.arange(HD // 2).astype(jnp.float32) * 2.0 / HD))
-    phases = positions * inverse_rate[None, :]
-    cosine, sine = jnp.cos(phases), jnp.sin(phases)
-    limits = jnp.tile(limits.astype(jnp.float32), (step_count, 1))
-    aux = jnp.concatenate(
-        [cosine, cosine, -sine, sine, jnp.pad(limits, ((0, 0), (0, 128 - prefix_count)))], axis=1
-    )
-    chosen = jnp.swapaxes(routes, 0, 1).reshape(rows, TOPK)
-    gates = jnp.sum(
-        jnp.where(
-            chosen[:, :, None] == jnp.arange(128)[None, None, :],
-            gate_weights.reshape(rows, TOPK)[:, :, None],
-            0.0,
-        ),
-        axis=1,
-    )
+    rates = jnp.tile(inverse_rate, 2).reshape(1, HD)
     in_vmem = pl.BlockSpec(memory_space=pltpu.VMEM)
+    in_smem = pl.BlockSpec(memory_space=pltpu.SMEM)
     in_hbm = pl.BlockSpec(memory_space=pl.ANY)
     everyone = n * rows
     bf16, f32 = jnp.bfloat16, jnp.float32
@@ -647,22 +688,28 @@
             jax.ShapeDtypeStruct((rows, width), f32),
             jax.ShapeDtypeStruct((rows, 2 * kv_width), bf16),
         ),
-        in_specs=[in_vmem] * 8 + [in_hbm] * 5,
+        in_specs=[in_vmem] * 4 + [in_smem] * 2 + [in_vmem] * 2 + [in_hbm] * 8,
         out_specs=(in_vmem, in_vmem),
         scratch_shapes=[
-            pltpu.VMEM((width, 256), bf16),
+            pltpu.VMEM((width, 128), bf16),
+            pltpu.VMEM((32, width), bf16),
+            pltpu.VMEM((rows, 128), f32),
+            pltpu.VMEM((rows, 128), f32),
+            pltpu.VMEM((everyone // 2, width), bf16),
+            pltpu.VMEM((rows, width), f32),
+            pltpu.VMEM((rows, width), f32),
             pltpu.VMEM((everyone, width), bf16),
             pltpu.VMEM((everyone, width), bf16),
             pltpu.VMEM((everyone, width), bf16),
-            pltpu.VMEM((everyone, 256), f32),
-            pltpu.VMEM((everyone, 256), f32),
+            pltpu.VMEM((n, rows + 8, 128), f32),
+            pltpu.VMEM((n, rows + 8, 128), f32),
             pltpu.VMEM((width, 128), bf16),
             pltpu.VMEM((everyone, 128), f32),
             pltpu.VMEM((everyone, 128), f32),
             pltpu.VMEM((rows, width), f32),
             pltpu.VMEM((everyone // 2, ff), bf16),
             pltpu.VMEM((everyone, width), bf16),
-            pltpu.VMEM((everyone, width), bf16),
+            pltpu.VMEM((everyone // 2, width), bf16),
             pltpu.VMEM((rows, kv_width), f32),
             pltpu.VMEM((rows, kv_width), f32),
             pltpu.VMEM((HQ * rows, HD), bf16),
@@ -670,11 +717,11 @@
             pltpu.VMEM((ff, width), bf16),
             pltpu.VMEM((prefix_count, span, kv_width), bf16),
             pltpu.VMEM((prefix_count, span, kv_width), bf16),
-            pltpu.SemaphoreType.DMA((5,)),
+            pltpu.SemaphoreType.DMA((8,)),
             pltpu.SemaphoreType.DMA((3, 16)),
             pltpu.SemaphoreType.DMA((3, 16)),
-            pltpu.SemaphoreType.DMA((4, 16)),
-            pltpu.SemaphoreType.DMA((4, 16)),
+            pltpu.SemaphoreType.DMA((6, 16)),
+            pltpu.SemaphoreType.DMA((6, 16)),
         ],
         compiler_params=pltpu.CompilerParams(
             collective_id=0, has_side_effects=True, vmem_limit_bytes=56 * 1024 * 1024
@@ -683,11 +730,14 @@
         states.reshape(rows, width),
         attn_gain.reshape(1, width),
         moe_gain.reshape(1, width),
+        rates,
+        cache_lengths,
+        prefix_slot,
+        routes,
+        gate_weights,
         w_query,
-        w_key,
-        w_value,
-        aux,
-        gates,
+        w_key.T,
+        w_value.T,
         w_output,
         w_gate_up[0],
         w_down[0],

time: 121 us -> 101 us (0.83)
  the two profiles are of different devices: /device:TPU:23 before, /device:TPU:0 now
where the time goes in v2:
time: 101 us
  Pallas kernels  96.8 us (96%)
  local copies, waits for them, and re-layouts  3.49 us (3%)
    pallas_call x1, Pallas kernels, tuned(): pl.pallas_call(layer_kernel, out_shape=(jax.ShapeDtypeStruct((rows, width...  96.8 us
    unnamed x2, local copies, waits for them, and re-layouts  2.89 us

profile of v2, /device:TPU:0, one launch (start us, length us, event | category | flops | bytes accessed | tf_op | source)
XLA Modules:
  0.0 100.9 jit_solution(7542205225064380062)
XLA Ops:
  0.7 0.6 reshape_tile.3.rates
  1.2 96.8 %shard_map.158 = (f32[16,2048]{1,0:T(8,128)}, bf16[16,512]{1,0:T(8,128)(2,1)}) custom-call(f32[16,2048]{1,0:T(8,128)} %bitcast.12, f32[1,2048]{1,0:T(1,128)} %bitcast.16, f32[1,2048]{1,0:T(1,128)} %bitcast.17, f32[1,128]{1,0:T(1,128)} %reshape_tile.3.rates, s32[2]{0:T(128)} %lengths.1, s32[8]{0:T(128)} %slots.1, s32[8,2,8]{2,1,0:T(2,128)} %routes.1, ...), custom_call_target="tpu_custom_call" | custom-call | tf_op jit(solution)/shard_map/pallas_call | solution.py:685
  98.1 1.6 %copy.19 = f32[2,8,2048]{2,1,0:T(8,128)} copy(f32[2,8,2048]{2,1,0:T(8,128)} %bitcast.11) | data formatting | bytes 262144
  99.6 1.3 %copy.20 = bf16[2,8,512]{2,1,0:T(8,128)(2,1)} copy(bf16[2,8,512]{2,1,0:T(8,128)(2,1)} %bitcast.15) | data formatting | bytes 32768
  (2 shorter events, 0.0 us)

commit v3 on v2

--- a/solution.py
+++ b/solution.py
@@ -348,16 +348,22 @@
             self.push(src, index_of(z, 1 - y, c))
             self.push(src, index_of(z, y, 1 - c))
 
-        def ready(self, shift):
+        def pass_on(self, shift):
             self.from_z(shift)
             self.from_y(z, shift)
             if shift == 0:
                 self.arrived(mirror)
                 self.spread(mirror)
+
+        def settle(self, shift):
             self.from_y(z_pair, shift)
             for zz in (z, z_pair):
                 for yy in (y, 1 - y):
                     self.arrived((index_of(zz, yy, 1 - c) + shift) % n)
+
+        def ready(self, shift):
+            self.pass_on(shift)
+            self.settle(shift)
 
         def finish(self):
             for copy in self.sends:
@@ -453,11 +459,13 @@
 
     project(near)
     scatter(parts, own_parts, 0, near, True)
+    for i in range(half):
+        w_copy((1 - near) * half + (me + i) % half, me).start()
     first.ready(half)
     project(1 - near)
     scatter(parts, own_parts, 0, 1 - near, False)
-    for i in range(1, n):
-        w_copy((me + i) % n, me).start()
+    for i in range(1, half):
+        w_copy(near * half + (me + i) % half, me).start()
     first.finish()
     scatter_wait(parts, own_parts, 0)
 
@@ -581,8 +589,10 @@
             )
             act[:, pl.ds(at, 256)] = (g / (1.0 + jnp.exp(-g)) * u).astype(jnp.bfloat16)
 
-    def down(group):
-        @pl.loop(0, down_v.shape[1] // 512)
+    def down(group, part):
+        tiles = down_v.shape[1] // 1024
+
+        @pl.loop(part * tiles, (part + 1) * tiles)
         def _(t):
             at = pl.multiple_of(t * 512, 512)
             expert_out[group_rows(group), pl.ds(at, 512)] = jnp.dot(
@@ -591,7 +601,30 @@
 
     third.ready(0)
     gate_up(near)
-    down(near)
+    third.pass_on(half)
+    down(near, 0)
+    down(near, 1)
+    third.settle(half)
+    gate_up(1 - near)
+    wide = down_v.shape[1] // 2
+
+    def strip(ref, i, part):
+        rows = pl.ds(pl.multiple_of(i * ROWS, ROWS), ROWS)
+        return ref.at[rows, part * wide : (part + 1) * wide]
+
+    def relayed(part, mate, landing):
+        return rdma(
+            strip(expert_out, (mate + half) % n, part),
+            strip(relay, landing % half, part),
+            a2a_send.at[4 + 2 * part, mate],
+            a2a_recv.at[4 + 2 * part, landing],
+            mate,
+        )
+
+    for part in range(2):
+        down(1 - near, part)
+        for i in range(1, half):
+            relayed(part, near * half + (me + i) % half, me).start()
     for i in range(1, half):
         mate = near * half + (me + i) % half
         rdma(
@@ -601,56 +634,55 @@
             a2a_recv.at[2, me],
             mate,
         ).start()
-    third.ready(half)
-    gate_up(1 - near)
-    down(1 - near)
-    for i in range(1, half):
-        mate = near * half + (me + i) % half
-        rdma(
-            block(expert_out, (mate + half) % n),
-            block(relay, me % half),
-            a2a_send.at[4, mate],
-            a2a_recv.at[4, me],
-            mate,
-        ).start()
     third.finish()
 
     def mixed(total, shares, e, got):
         share = jnp.sum(jnp.where(lane_id == e, shares[...], 0.0), axis=1, keepdims=True)
         return total + jnp.where(share > 0.0, share * got[...].astype(jnp.float32), 0.0)
 
-    def mix(total, shares, phase, buf):
+    gates_copy.wait()
+    sums = []
+    for part in range(2):
+        total = mixed(
+            jnp.zeros((ROWS, wide), jnp.float32), mirror_gates, me, strip(expert_out, mirror, part)
+        )
         for i in range(1, half):
             e = near * half + (me + i) % half
-            rdma(
-                block(expert_out, e),
-                block(buf, e % half),
-                a2a_send.at[phase, e],
-                a2a_recv.at[phase, e],
-                e,
-            ).wait_recv()
-            total = mixed(total, shares, e, block(buf, e % half))
-        return total
-
-    gates_copy.wait()
-    total = mixed(jnp.zeros(hidden.shape, jnp.float32), mirror_gates, me, block(expert_out, mirror))
-    summed[...] = mix(total, mirror_gates, 4, relay)
-    sum_copy = rdma(summed, from_mirror, a2a_send.at[5, 0], a2a_recv.at[5, 0], mirror)
-    sum_copy.start()
+            relayed(part, e, e).wait_recv()
+            total = mixed(total, mirror_gates, e, strip(relay, e % half, part))
+        strip(summed, 0, part)[...] = total
+        copy = rdma(
+            strip(summed, 0, part),
+            strip(from_mirror, 0, part),
+            a2a_send.at[5, 2 + part],
+            a2a_recv.at[5, 2 + part],
+            mirror,
+        )
+        copy.start()
+        sums.append(copy)
+
+    def back(e):
+        return rdma(
+            block(expert_out, e),
+            block(returned, e % half),
+            a2a_send.at[2, e],
+            a2a_recv.at[2, e],
+            e,
+        )
+
     total = mixed(hidden[...], gates, me, block(expert_out, me))
-    total = mix(total, gates, 2, returned)
-    sum_copy.wait()
+    for i in range(1, half):
+        e = near * half + (me + i) % half
+        back(e).wait_recv()
+        total = mixed(total, gates, e, block(returned, e % half))
+    for copy in sums:
+        copy.wait()
     out[...] = total + from_mirror[...]
-    for phase, buf in ((2, returned), (4, relay)):
-        for i in range(1, half):
-            e = near * half + (me + i) % half
-            rdma(
-                block(expert_out, e),
-                block(buf, e % half),
-                a2a_send.at[phase, e],
-                a2a_recv.at[phase, e],
-                e,
-            ).wait_send()
+    for i in range(1, half):
+        e = near * half + (me + i) % half
+        back(e).wait_send()
+        for part in range(2):
+            relayed(part, e, e).wait_send()
 
 
 def tuned(
@@ -720,8 +752,8 @@
             pltpu.SemaphoreType.DMA((8,)),
             pltpu.SemaphoreType.DMA((3, 16)),
             pltpu.SemaphoreType.DMA((3, 16)),
-            pltpu.SemaphoreType.DMA((6, 16)),
-            pltpu.SemaphoreType.DMA((6, 16)),
+            pltpu.SemaphoreType.DMA((7, 16)),
+            pltpu.SemaphoreType.DMA((7, 16)),
         ],
         compiler_params=pltpu.CompilerParams(
             collective_id=0, has_side_effects=True, vmem_limit_bytes=56 * 1024 * 1024

time: 101 us -> 94.3 us (0.934)
  Pallas kernels: 96.8 us -> 89.3 us
    pallas_call x1, Pallas kernels: 96.8 us -> 89.3 us  [tuned(): pl.pallas_call(layer_kernel, out_shape=(jax.ShapeDtypeStruct((rows, width...]
where the time goes in v3:
time: 94.3 us; the launch traced here: 93.5 us
  Pallas kernels  89.3 us (95%)
  local copies, waits for them, and re-layouts  3.49 us (4%)
    pallas_call x1, Pallas kernels, tuned(): pl.pallas_call(layer_kernel, out_shape=(jax.ShapeDtypeStruct((rows, width...  89.3 us
    unnamed x2, local copies, waits for them, and re-layouts  2.89 us

profile of v3, /device:TPU:0, one launch (start us, length us, event | category | flops | bytes accessed | tf_op | source)
XLA Modules:
  0.0 93.5 jit_solution(10838001413957440239)
XLA Ops:
  0.7 0.6 reshape_tile.3.rates
  1.2 89.3 %shard_map.158 = (f32[16,2048]{1,0:T(8,128)}, bf16[16,512]{1,0:T(8,128)(2,1)}) custom-call(f32[16,2048]{1,0:T(8,128)} %bitcast.12, f32[1,2048]{1,0:T(1,128)} %bitcast.16, f32[1,2048]{1,0:T(1,128)} %bitcast.17, f32[1,128]{1,0:T(1,128)} %reshape_tile.3.rates, s32[2]{0:T(128)} %lengths.1, s32[8]{0:T(128)} %slots.1, s32[8,2,8]{2,1,0:T(2,128)} %routes.1, ...), custom_call_target="tpu_custom_call" | custom-call | tf_op jit(solution)/shard_map/pallas_call | solution.py:717
  90.6 1.6 %copy.19 = f32[2,8,2048]{2,1,0:T(8,128)} copy(f32[2,8,2048]{2,1,0:T(8,128)} %bitcast.11) | data formatting | bytes 262144
  92.1 1.3 %copy.20 = bf16[2,8,512]{2,1,0:T(8,128)(2,1)} copy(bf16[2,8,512]{2,1,0:T(8,128)(2,1)} %bitcast.15) | data formatting | bytes 32768
  (2 shorter events, 0.0 us)
